TPU v7x, 256 devices: a whole 4x4x8 slice. The times are simulated.
256 devices in a mesh: row: 32 (over y, z), col: 8 (over x, core).
Axes of the slice: x: 4, y: 4, z: 8, core: 2. Of those that a mesh axis runs over, the one named last changes fastest.
Arguments:
- blocks: bfloat16 [4096, 3, 128, 128], P(('row', 'col')), may hold values from -0.3984375 to 0.3984375
- rows: int32 [4096, 3], P(('row', 'col')), may hold values from 0 to 63, as said below
- counts: int32 [4096], P(('row', 'col')), may hold values from 1 to 3
- sketch: bfloat16 [524288, 128], P(('row', 'col')), may hold values from -6 to 6
- weights: float32 [8192], replicated, may hold values from 0.35 to 2.8
Outputs:
- basis_out: float32 [8192, 128], P(('row', 'col'))
- right_factors: bfloat16 [524288, 128], P(('row', 'col'))
Inputs may be any that keep to these rules, and one draw needn't show every extreme that they name: `rows`: the 3 entries of each document block are distinct feature blocks.
All inputs are finite; a program needn't handle non-finite values.
Results may differ from a plain program's by a relative error of at most 0.0049.
Values may be sent and summed in bfloat16 or wider, within the bound.
A program may use at most 64 MiB of HBM per device.

v0:
```python
import jax
import jax.numpy as jnp
from jax import lax
from jax.sharding import PartitionSpec as P

HIGHEST = lax.Precision.HIGHEST


def body(blocks, rows, counts, sketch, weights):
    doc_blocks = blocks.shape[0]
    slot_count = blocks.shape[1]
    block_width = blocks.shape[2]
    columns = sketch.shape[1]
    features = weights.shape[0]
    feature_blocks = features // block_width
    in_use = lax.broadcasted_iota(jnp.int32, (doc_blocks, slot_count), 1) < counts[:, None]
    segment_ids = jnp.where(in_use, rows, feature_blocks).reshape(-1)
    row_count = lax.axis_size("row")
    col_count = lax.axis_size("col")
    flat_rows = features // (row_count * col_count)
    flat_index = lax.axis_index("row") * col_count + lax.axis_index("col")
    flat_start = flat_index * flat_rows
    flat_weights = lax.dynamic_slice_in_dim(weights, flat_start, flat_rows)[:, None]
    width_now = sketch.shape[1]
    tiles_docs = sketch.reshape(doc_blocks, block_width, width_now)
    terms = jnp.einsum("dsfk,dkl->dsfl", blocks, tiles_docs, preferred_element_type=jnp.float32)
    terms = terms.reshape(doc_blocks * slot_count, block_width, width_now)
    summed = jax.ops.segment_sum(terms, segment_ids, num_segments=feature_blocks + 1)
    local_terms = summed[:feature_blocks].reshape(features, sketch.shape[1])
    flat_summed = (
        lax.psum_scatter(local_terms, ("row", "col"), scatter_dimension=0, tiled=True)
        * flat_weights
    )
    chol_factor = jnp.linalg.cholesky(
        lax.psum(jnp.dot(flat_summed.T, flat_summed, precision=HIGHEST), ("row", "col")) / features
    )
    inverse = jax.scipy.linalg.solve_triangular(
        chol_factor, jnp.eye(columns, dtype=jnp.float32), lower=True
    )
    current = jnp.dot(flat_summed, inverse.T, precision=HIGHEST)
    weighted = (current * flat_weights).astype(jnp.bfloat16)
    gathered = lax.all_gather(weighted, ("row", "col"), axis=0, tiled=True)
    width_now = gathered.shape[1]
    picked = gathered.reshape(feature_blocks, block_width, width_now)[rows]
    picked = jnp.where(in_use[:, :, None, None], picked, jnp.zeros((), gathered.dtype))
    product = jnp.einsum("dsfl,dsfk->dkl", picked, blocks, preferred_element_type=jnp.float32)
    factors = product.reshape(doc_blocks * block_width, width_now).astype(jnp.bfloat16)
    return (current, factors)


def solution(mesh):
    placed = (
        P(("row", "col"), None, None, None),
        P(("row", "col"), None),
        P(("row", "col")),
        P(("row", "col"), None),
        P(),
    )
    return jax.shard_map(
        body,
        mesh=mesh,
        in_specs=placed,
        out_specs=(P(("row", "col"), None), P(("row", "col"), None)),
        check_vma=False,
    )
```

profile of v0, /device:TPU:1, one launch (start us, length us, event | category | flops | bytes accessed | tf_op | source)
XLA Modules:
  0.0 1698.7 jit_solution(12156809714150162819)
XLA Ops:
  7.2 0.0 copy-start
  7.2 0.0 reduce-scatter.2.cloned.1.call-start
  7.2 0.8 compare_select_fusion
  8.0 0.1 copy.13
  8.1 0.1 reshape.61
  8.2 0.4 copy-done
  8.6 3.3 fusion.21
  11.9 2.5 broadcast_in_dim.27
  14.4 10.1 scatter_fusion
  24.5 4.7 slice.18
  29.2 0.0 copy-start.1
  29.2 0.0 reduce-scatter.2.cloned.1.call-update
  29.2 0.0 all-reduce.2.cloned.1.call-start
  29.2 0.8 dynamic_slice.3
  30.0 1285.1 %reduce-scatter.2.cloned.1.call-done = f32[32,128]{1,0:T(8,128)} async-done(((f32[8192,128]{1,0:T(8,128)}), f32[32,128]{1,0:T(8,128)}) %reduce-scatter.2.cloned.1.call-update) | async-done | bytes 16400 | tf_op jit(solution)/shard_map/reduce_scatter | solution.py:31
  1315.1 1.8 fusion.16
  1316.9 0.0 all-reduce.2.cloned.1.call-update
  1316.9 0.0 all-gather.2.cloned.1.call-start
  1317.0 243.9 %all-reduce.2.cloned.1.call-done = f32[128,128]{0,1:T(8,128)} async-done(((f32[128,128]{0,1:T(8,128)}), f32[128,128]{0,1:T(8,128)}) %all-reduce.2.cloned.1.call-update) | async-done | bytes 65552 | tf_op jit(solution)/shard_map/psum | solution.py:35
  1560.9 0.8 broadcast_multiply_fusion
  1561.7 0.1 copy.15
  1561.8 0.9 fusion.13
  1562.7 11.7 cholesky.17
  1574.4 0.6 compare_reduce_fusion
  1575.1 0.7 fusion.10
  1575.7 9.8 custom-call.7
  1585.5 0.2 fusion.11
  1585.8 1.6 multiply_convert_fusion
  1587.4 0.0 all-gather.2.cloned.1.call-update
  1587.4 0.1 copy.17
  1587.5 0.1 reshape.53
  1587.6 0.0 copy-done.1
  1587.6 0.1 copy.16
  1587.7 100.5 %all-gather.2.cloned.1.call-done = bf16[8192,128]{1,0:T(8,128)(2,1)} async-done(((bf16[32,128]{1,0:T(8,128)(2,1)}), bf16[8192,128]{1,0:T(8,128)(2,1)}) %all-gather.2.cloned.1.call-update) | async-done | bytes 2097168 | tf_op jit(solution)/shard_map/all_gather | solution.py:42
  1688.2 2.4 gather_fusion
  1690.7 1.5 fusion.6
  (3 shorter events, 0.0 us)
Async XLA Ops:
  7.2 1.4 copy-start
  7.2 1308.0 %reduce-scatter.2.cloned.1.call-start = ((), (), s32[]{:S(2)}) async-start(), calls=%async_computation.1 | async-start | bytes 4210688 | tf_op jit(solution)/shard_map/reduce_scatter | solution.py:31
  29.2 1558.4 %copy-start.1 = (s32[16]{0:T(128)S(1)}, s32[16]{0:T(128)}, u32[]{:S(2)}) copy-start(s32[16]{0:T(128)} %param.7) | copy-start | bytes 196
  29.2 1531.7 %all-reduce.2.cloned.1.call-start = ((), (), s32[]{:S(2)}) async-start(), calls=%async_computation.2 | async-start | bytes 131072 | tf_op jit(solution)/shard_map/psum | solution.py:35
  1316.9 371.3 %all-gather.2.cloned.1.call-start = ((), (), s32[]{:S(2)}) async-start(), calls=%async_computation.3 | async-start | bytes 2105344 | tf_op jit(solution)/shard_map/all_gather | solution.py:42
Sparse Core Ops, SparseCore 0:
  29.3 1285.7 reduce-scatter.1
  1321.2 239.5 all-reduce.1
  1587.5 100.6 all-gather.1
where the time goes:
time: 1700 us
  waiting for transfers between devices  1630 us (96%)
  other arithmetic  35.5 us (2%)
    reduce_scatter x1, waiting for transfers between devices, body(): lax.psum_scatter(local_terms, ('row', 'col'), scatter_dimension=0, tiled=...  1290 us
    psum x1, waiting for transfers between devices, body(): lax.psum(jnp.dot(flat_summed.T, flat_summed, precision=HIGHEST), ('row',...  244 us
    all_gather x1, waiting for transfers between devices, body(): gathered = lax.all_gather(weighted, ('row', 'col'), axis=0, tiled=True)  101 us
  transfers between devices with their start and end apart: 3, of which 3 were waited for; matrix products, arithmetic and copies ran while one was open for 0% of the time, Pallas kernels for 0%

commit v1 on v0

--- a/solution.py
+++ b/solution.py
@@ -32,7 +32,8 @@
         * flat_weights
     )
     chol_factor = jnp.linalg.cholesky(
-        lax.psum(jnp.dot(flat_summed.T, flat_summed, precision=HIGHEST), ("row", "col")) / features
+        lax.psum(lax.psum(jnp.dot(flat_summed.T, flat_summed, precision=HIGHEST), "col"), "row")
+        / features
     )
     inverse = jax.scipy.linalg.solve_triangular(
         chol_factor, jnp.eye(columns, dtype=jnp.float32), lower=True

time: 1700 us -> 1670 us (0.982)
  waiting for transfers between devices: 1630 us -> 1600 us
    psum x1 -> x2, waiting for transfers between devices: 244 us -> 203 us  [the longest x1 141 us: body(): lax.psum(lax.psum(jnp.dot(flat_summed.T, flat_summed, precision=HIGHEST),...]
  transfers between devices with their start and end apart: 3 -> 4, of which waited for: 3 -> 4; matrix products, arithmetic and copies ran while one was open for 0% -> 0% of each run, Pallas kernels for 0% -> 0%
where the time goes in v1:
time: 1670 us; the launch traced here: 1660 us
  waiting for transfers between devices  1600 us (96%)
  other arithmetic  35.5 us (2%)
    reduce_scatter x1, waiting for transfers between devices, body(): lax.psum_scatter(local_terms, ('row', 'col'), scatter_dimension=0, tiled=...  1290 us
    psum x1, waiting for transfers between devices, body(): lax.psum(lax.psum(jnp.dot(flat_summed.T, flat_summed, precision=HIGHEST),...  141 us
    all_gather x1, waiting for transfers between devices, body(): gathered = lax.all_gather(weighted, ('row', 'col'), axis=0, tiled=True)  107 us
    psum x1, waiting for transfers between devices, body(): lax.psum(jnp.dot(flat_summed.T, flat_summed, precision=HIGHEST), 'col')  61.7 us
  transfers between devices with their start and end apart: 4, of which 4 were waited for; matrix products, arithmetic and copies ran while one was open for 0% of the time, Pallas kernels for 0%

profile of v1, /device:TPU:1, one launch (start us, length us, event | category | flops | bytes accessed | tf_op | source)
XLA Modules:
  0.0 1664.4 jit_solution(5926269524902462967)
XLA Ops:
  7.2 0.0 copy-start
  7.2 0.0 reduce-scatter.2.cloned.1.call-start
  7.2 0.8 compare_select_fusion
  8.0 0.1 copy.13
  8.1 0.1 reshape.61
  8.2 0.4 copy-done
  8.6 3.3 fusion.21
  11.9 2.5 broadcast_in_dim.27
  14.4 10.1 scatter_fusion
  24.5 4.7 slice.18
  29.2 0.0 copy-start.1
  29.2 0.0 reduce-scatter.2.cloned.1.call-update
  29.2 0.0 all-reduce.3.cloned.1.call-start
  29.2 0.8 dynamic_slice.3
  30.0 1285.1 %reduce-scatter.2.cloned.1.call-done = f32[32,128]{1,0:T(8,128)} async-done(((f32[8192,128]{1,0:T(8,128)}), f32[32,128]{1,0:T(8,128)}) %reduce-scatter.2.cloned.1.call-update) | async-done | bytes 16400 | tf_op jit(solution)/shard_map/reduce_scatter | solution.py:31
  1315.1 1.8 fusion.16
  1316.9 0.0 all-reduce.3.cloned.1.call-update
  1316.9 0.0 all-reduce.5.cloned.1.call-start
  1317.0 61.7 %all-reduce.3.cloned.1.call-done = f32[128,128]{0,1:T(8,128)} async-done(((f32[128,128]{0,1:T(8,128)}), f32[128,128]{0,1:T(8,128)}) %all-reduce.3.cloned.1.call-update) | async-done | bytes 65552 | tf_op jit(solution)/shard_map/psum | solution.py:35
  1378.7 0.0 all-reduce.5.cloned.1.call-update
  1378.7 0.0 all-gather.2.cloned.1.call-start
  1378.7 141.5 %all-reduce.5.cloned.1.call-done = f32[128,128]{0,1:T(8,128)} async-done(((f32[128,128]{0,1:T(8,128)}), f32[128,128]{0,1:T(8,128)}) %all-reduce.5.cloned.1.call-update) | async-done | bytes 65552 | tf_op jit(solution)/shard_map/psum | solution.py:35
  1520.2 0.8 broadcast_multiply_fusion
  1521.1 0.1 copy.15
  1521.2 0.9 fusion.13
  1522.0 11.7 cholesky.17
  1533.8 0.6 compare_reduce_fusion
  1534.4 0.7 fusion.10
  1535.1 9.8 custom-call.7
  1544.9 0.2 fusion.11
  1545.1 1.6 multiply_convert_fusion
  1546.7 0.0 all-gather.2.cloned.1.call-update
  1546.7 0.1 copy.17
  1546.8 0.1 reshape.53
  1546.9 0.0 copy-done.1
  1546.9 0.1 copy.16
  1547.0 106.9 %all-gather.2.cloned.1.call-done = bf16[8192,128]{1,0:T(8,128)(2,1)} async-done(((bf16[32,128]{1,0:T(8,128)(2,1)}), bf16[8192,128]{1,0:T(8,128)(2,1)}) %all-gather.2.cloned.1.call-update) | async-done | bytes 2097168 | tf_op jit(solution)/shard_map/all_gather | solution.py:43
  1653.9 2.4 gather_fusion
  1656.4 1.5 fusion.6
  (3 shorter events, 0.0 us)
Async XLA Ops:
  7.2 1.4 copy-start
  7.2 1308.0 %reduce-scatter.2.cloned.1.call-start = ((), (), s32[]{:S(2)}) async-start(), calls=%async_computation.1 | async-start | bytes 4210688 | tf_op jit(solution)/shard_map/reduce_scatter | solution.py:31
  29.2 1517.8 %copy-start.1 = (s32[16]{0:T(128)S(1)}, s32[16]{0:T(128)}, u32[]{:S(2)}) copy-start(s32[16]{0:T(128)} %param.7) | copy-start | bytes 196
  29.2 1349.5 %all-reduce.3.cloned.1.call-start = ((), (), s32[]{:S(2)}) async-start(), calls=%async_computation.2 | async-start | bytes 131072 | tf_op jit(solution)/shard_map/psum | solution.py:35
  1316.9 203.3 %all-reduce.5.cloned.1.call-start = ((), (), s32[]{:S(2)}) async-start(), calls=%async_computation.3 | async-start | bytes 131072 | tf_op jit(solution)/shard_map/psum | solution.py:35
  1378.7 275.2 %all-gather.2.cloned.1.call-start = ((), (), s32[]{:S(2)}) async-start(), calls=%async_computation.4 | async-start | bytes 2105344 | tf_op jit(solution)/shard_map/all_gather | solution.py:43
Sparse Core Ops, SparseCore 0:
  29.3 1285.7 reduce-scatter.1
  1318.0 60.6 all-reduce.2
  1382.1 138.0 all-reduce.4
  1546.9 107.0 all-gather.1

commit v2 on v0

--- a/solution.py
+++ b/solution.py
@@ -32,7 +32,11 @@
         * flat_weights
     )
     chol_factor = jnp.linalg.cholesky(
-        lax.psum(jnp.dot(flat_summed.T, flat_summed, precision=HIGHEST), ("row", "col")) / features
+        jnp.sum(
+            lax.all_gather(jnp.dot(flat_summed.T, flat_summed, precision=HIGHEST), ("row", "col")),
+            axis=0,
+        )
+        / features
     )
     inverse = jax.scipy.linalg.solve_triangular(
         chol_factor, jnp.eye(columns, dtype=jnp.float32), lower=True

time: 1700 us -> 1590 us (0.935)
  waiting for transfers between devices: 1630 us -> 1510 us
    psum x1 -> x0, waiting for transfers between devices: 244 us -> none  [body(): lax.psum(jnp.dot(flat_summed.T, flat_summed, precision=HIGHEST), ('row',...]
    all_gather x0 -> x1, waiting for transfers between devices: none -> 126 us  [body(): lax.all_gather(jnp.dot(flat_summed.T, flat_summed, precision=HIGHEST), ('...]
where the time goes in v2:
time: 1590 us
  waiting for transfers between devices  1510 us (95%)
  other arithmetic  40.4 us (3%)
    reduce_scatter x1, waiting for transfers between devices, body(): lax.psum_scatter(local_terms, ('row', 'col'), scatter_dimension=0, tiled=...  1290 us
    all_gather x1, waiting for transfers between devices, body(): lax.all_gather(jnp.dot(flat_summed.T, flat_summed, precision=HIGHEST), ('...  126 us
    all_gather x1, waiting for transfers between devices, body(): gathered = lax.all_gather(weighted, ('row', 'col'), axis=0, tiled=True)  101 us
  transfers between devices with their start and end apart: 3, of which 3 were waited for; matrix products, arithmetic and copies ran while one was open for 0% of the time, Pallas kernels for 0%

profile of v2, /device:TPU:1, one launch (start us, length us, event | category | flops | bytes accessed | tf_op | source)
XLA Modules:
  0.0 1585.3 jit_solution(1175515840141625858)
XLA Ops:
  7.2 0.0 copy-start
  7.2 0.0 reduce-scatter.2.cloned.1.call-start
  7.2 0.8 compare_select_fusion
  8.0 0.1 copy.17
  8.1 0.1 reshape.61
  8.2 0.4 copy-done
  8.6 3.3 fusion.21
  11.9 2.5 broadcast_in_dim.27
  14.4 10.1 scatter_fusion
  24.5 4.7 slice.18
  29.2 0.0 reduce-scatter.2.cloned.1.call-update
  29.2 0.0 all-gather.6.cloned.1.call-start
  29.2 0.8 dynamic_slice.3
  30.0 1285.1 %reduce-scatter.2.cloned.1.call-done = f32[32,128]{1,0:T(8,128)} async-done(((f32[8192,128]{1,0:T(8,128)}), f32[32,128]{1,0:T(8,128)}) %reduce-scatter.2.cloned.1.call-update) | async-done | bytes 16400 | tf_op jit(solution)/shard_map/reduce_scatter | solution.py:31
  1315.1 1.8 fusion.16
  1316.9 0.0 all-gather.6.cloned.1.call-update
  1316.9 0.0 all-gather.4.cloned.1.call-start
  1317.0 125.8 %all-gather.6.cloned.1.call-done = f32[32768,128]{1,0:T(8,128)} async-done(((f32[128,128]{1,0:T(8,128)}), f32[32768,128]{1,0:T(8,128)}) %all-gather.6.cloned.1.call-update) | async-done | bytes 16777232 | tf_op jit(solution)/shard_map/all_gather | solution.py:36
  1442.8 0.0 copy-start.1
  1442.8 0.0 copy-start.2
  1442.8 6.6 reduce_sum.11
  1449.4 0.1 copy.18
  1449.5 11.7 cholesky.17
  1461.2 0.6 compare_reduce_fusion
  1461.9 0.7 fusion.10
  1462.5 9.8 custom-call.7
  1472.4 0.2 fusion.11
  1472.6 0.0 copy-done.1
  1472.6 0.9 multiply_convert_fusion
  1473.5 0.0 all-gather.4.cloned.1.call-update
  1473.5 0.1 copy.20
  1473.6 0.1 reshape.53
  1473.7 0.0 copy-done.2
  1473.7 0.1 copy.19
  1473.8 101.0 %all-gather.4.cloned.1.call-done = bf16[8192,128]{1,0:T(8,128)(2,1)} async-done(((bf16[32,128]{1,0:T(8,128)(2,1)}), bf16[8192,128]{1,0:T(8,128)(2,1)}) %all-gather.4.cloned.1.call-update) | async-done | bytes 2097168 | tf_op jit(solution)/shard_map/all_gather | solution.py:46
  1574.8 2.4 gather_fusion
  1577.3 1.5 fusion.6
  (4 shorter events, 0.1 us)
Async XLA Ops:
  7.2 1.4 copy-start
  7.2 1308.0 %reduce-scatter.2.cloned.1.call-start = ((), (), s32[]{:S(2)}) async-start(), calls=%async_computation.1 | async-start | bytes 4210688 | tf_op jit(solution)/shard_map/reduce_scatter | solution.py:31
  29.2 1413.6 %all-gather.6.cloned.1.call-start = ((), (), s32[]{:S(2)}) async-start(), calls=%async_computation.3 | async-start | bytes 16842752 | tf_op jit(solution)/shard_map/all_gather | solution.py:36
  1316.9 257.9 %all-gather.4.cloned.1.call-start = ((), (), s32[]{:S(2)}) async-start(), calls=%async_computation.2 | async-start | bytes 2105344 | tf_op jit(solution)/shard_map/all_gather | solution.py:46
  1442.8 29.9 %copy-start.1 = (f32[32,128]{1,0:T(8,128)S(1)}, f32[32,128]{1,0:T(8,128)}, u32[]{:S(2)}) copy-start(f32[32,128]{1,0:T(8,128)} %reduce-scatter.2.cloned.1.call-done) | copy-start | bytes 49156
  1442.8 30.9 %copy-start.2 = (s32[16]{0:T(128)S(1)}, s32[16]{0:T(128)}, u32[]{:S(2)}) copy-start(s32[16]{0:T(128)} %param.7) | copy-start | bytes 196
Sparse Core Ops, SparseCore 0:
  29.3 1285.7 reduce-scatter.1
  1319.3 123.4 all-gather.5
  1473.6 101.1 all-gather.3
